TPU v7x, 512 devices: a whole 4x8x8 slice. The times are simulated.
512 devices in a mesh: tile: 64 (over y, x, core), view: 8 (over z).
Axes of the slice: x: 4, y: 8, z: 8, core: 2. Of those that a mesh axis runs over, the one named last changes fastest.
Arguments:
- volume: float32 [64, 512, 512], P(None, 'tile'), may hold values from 0.09 to 7.2
- weights: bfloat16 [64, 32, 32, 48, 256], P('tile', 'view'), may hold values from 0 to 0.0546875
- measured: float32 [64, 8, 1, 64, 48], P('tile', 'view'), may hold values from 4 to 40
- crossings: int32 [64, 32, 32, 2], P('tile', 'view'), may hold values from 0 to 15, as said below
- counts: int32 [64, 32], P('tile', 'view'), may hold values from 16 to 32
Outputs:
- updated: float32 [64, 512, 512], P(None, 'tile')
Inputs may be any that keep to these rules, and one draw needn't show every extreme that they name: `crossings`: slots follow a parallel-beam geometry: each segment of a strip has one or two live slots, naming the one or two adjacent blocks that its pixels' footprints reach in that view; the live slots of a strip and view come first; a dead slot repeats the first block of its segment.
All inputs are finite; a program needn't handle non-finite values.
Results may differ from a plain program's by a relative error of at most 0.002.
Values may be sent and summed in bfloat16 or wider, within the bound.
A program may use at most 64 MiB of HBM per device.

v0:
```python
import jax
import jax.numpy as jnp
from jax import lax
from jax.sharding import PartitionSpec as P

BACKGROUND = 1.0
HUBER_DELTA = 0.1


def extended(x, sides, width):
    for axis, dim in sides:
        peers, length = (lax.axis_size(axis), x.shape[dim])
        up = [(i, (i + 1) % peers) for i in range(peers - 1)]
        down = [(j, i) for i, j in up]
        last = lax.slice_in_dim(x, length - width, length, axis=dim)
        initial = lax.slice_in_dim(x, 0, width, axis=dim)
        before = lax.ppermute(last, axis, up)
        after = lax.ppermute(initial, axis, down)
        x = jnp.concatenate([before, x, after], axis=dim)
    return x


def per_device(volume, weights, measured, crossings, counts):
    high = lax.Precision.HIGHEST
    tile_count = lax.axis_size("tile")
    view_local = weights.shape[1]
    slot_count = weights.shape[2]
    bin_count = weights.shape[3]
    seg_pixels = weights.shape[4]
    plane_count = volume.shape[0]
    row_count = volume.shape[1]
    col_count = volume.shape[2]
    seg_cols = seg_pixels // row_count
    seg_total = col_count // seg_cols
    owned = measured.shape[2]
    blocks_view = owned * tile_count // view_local
    block_total = tile_count * owned
    slot_total = view_local * slot_count
    flat_width = plane_count * bin_count
    slot_weights = weights.reshape(slot_total, bin_count, seg_pixels)
    block_of = crossings[0, :, :, 0].reshape(slot_total)
    segment_of = crossings[0, :, :, 1].reshape(slot_total)
    alive = (jnp.arange(slot_count, dtype=jnp.int32)[None, :] < counts[0][:, None]).reshape(
        slot_total
    )
    alive_f = alive.astype(jnp.float32)
    view_slot = jnp.arange(slot_total, dtype=jnp.int32) // slot_count
    global_block = view_slot * blocks_view + block_of
    block_onehot = (
        global_block[:, None] == jnp.arange(block_total, dtype=jnp.int32)[None, :]
    ).astype(jnp.float32)
    block_onehot = block_onehot * alive_f[:, None]
    segment_onehot = (
        segment_of[:, None] == jnp.arange(seg_total, dtype=jnp.int32)[None, :]
    ).astype(jnp.float32)
    segments = volume.astype(jnp.bfloat16).reshape(plane_count, row_count, seg_total, seg_cols)
    segments = segments.transpose(0, 2, 1, 3).reshape(plane_count, seg_total, seg_pixels)
    slot_volume = jnp.einsum(
        "sq,pqx->spx",
        segment_onehot.astype(jnp.bfloat16),
        segments,
        preferred_element_type=jnp.float32,
    ).astype(jnp.bfloat16)
    partial_value = jnp.einsum(
        "spx,snx->spn", slot_volume, slot_weights, preferred_element_type=jnp.float32
    )
    dense = jnp.dot(block_onehot.T, partial_value.reshape(slot_total, flat_width), precision=high)
    dense = dense.reshape(tile_count, owned, flat_width)
    projection = lax.psum_scatter(dense, "tile", scatter_dimension=0, tiled=True)[0]
    ratios = (measured[0, 0].reshape(owned, flat_width) / (projection + BACKGROUND)).astype(
        jnp.bfloat16
    )
    every_block = lax.all_gather(ratios, "tile", axis=0, tiled=True)
    picked = jnp.dot(
        block_onehot.astype(jnp.bfloat16), every_block, preferred_element_type=jnp.float32
    ).astype(jnp.bfloat16)
    picked = picked.reshape(slot_total, plane_count, bin_count)
    spread_back = jnp.einsum(
        "spn,snx->spx", picked, slot_weights, preferred_element_type=jnp.float32
    )
    back_sum = jnp.einsum("sq,spx->pqx", segment_onehot, spread_back, precision=high)
    back_sum = back_sum.reshape(plane_count, seg_total, row_count, seg_cols).transpose(0, 2, 1, 3)
    back_sum = back_sum.reshape(volume.shape)
    live_segments = (segment_onehot * alive_f[:, None]).astype(jnp.bfloat16)
    sensitivity = jnp.einsum(
        "sq,snx->qx", live_segments, slot_weights, preferred_element_type=jnp.float32
    )
    sensitivity = (
        sensitivity.reshape(seg_total, row_count, seg_cols)
        .transpose(1, 0, 2)
        .reshape(row_count, col_count)
    )
    widened = extended(volume, (("tile", 1),), 1)
    padded = jnp.pad(widened, ((1, 1), (0, 0), (1, 1)))
    centre = padded[1:-1, 1:-1, 1:-1]
    penalty = jnp.zeros_like(volume)
    for other in (
        padded[2:, 1:-1, 1:-1],
        padded[:-2, 1:-1, 1:-1],
        padded[1:-1, 2:, 1:-1],
        padded[1:-1, :-2, 1:-1],
        padded[1:-1, 1:-1, 2:],
        padded[1:-1, 1:-1, :-2],
    ):
        penalty = penalty + jnp.clip(centre - other, -HUBER_DELTA, HUBER_DELTA)
    back_total, sens_total = lax.psum((back_sum, sensitivity), "view")
    return volume * back_total / (sens_total[None] * (1.0 + penalty))


def solution(mesh):
    in_specs = (
        P(None, "tile", None),
        P("tile", "view", None, None, None),
        P("tile", "view", None, None, None),
        P("tile", "view", None, None),
        P("tile", "view"),
    )
    out_specs = P(None, "tile", None)
    return jax.shard_map(
        per_device, mesh=mesh, in_specs=in_specs, out_specs=out_specs, check_vma=False
    )
```

profile of v0, /device:TPU:2, one launch (start us, length us, event | category | flops | bytes accessed | tf_op | source)
XLA Modules:
  0.0 397.6 jit_solution(3167328225006800716)
XLA Ops:
  6.5 0.0 all-reduce.7.cloned.1.call-start
  6.5 0.8 slice_reduce_fusion.1
  7.3 0.1 eq.31
  7.4 1.8 copy.79
  9.2 0.1 copy.80
  9.3 1.6 copy.81
  11.0 0.0 copy-start
  11.0 2.5 convolution_convert_fusion.1
  13.4 0.0 copy-done
  13.4 4.5 %fusion.2 = f32[128,64,48]{1,2,0:T(8,128)} fusion(bf16[128,48,256]{2,1,0:T(8,128)(2,1)S(1)} %bitcast.51, bf16[128,64,256]{2,0,1:T(8,128)(2,1)S(1)} %convolution_convert_fusion.1), kind=kOutput, calls=%fused_computation.3 | convolution fusion | flops 201326592 | bytes 8912896 | tf_op jit(solution)/shard_map/spx,snx->spn/dot_general | solution.py:64
  17.9 0.0 copy-start.2
  17.9 3.3 copy.83
  21.2 0.0 copy-start.1
  21.2 0.1 reshape_squeeze.6
  21.3 0.0 copy-done.2
  21.3 0.1 fusion.48
  21.3 0.1 reshape.107
  21.4 4.1 %convolution_bitcast_fusion = f32[64,1,3072]{2,0,1:T(8,128)} fusion(f32[128,3072]{0,1:T(8,128)} %bitcast.55, f32[128]{0:T(128)S(1)} %reshape.107, s32[128]{0:T(128)S(1)} %fusion.50), kind=kOutput, calls=%fused_computation.10 | convolution fusion | flops 302006272 | bytes 2360320 | tf_op jit(solution)/shard_map/dot_general | solution.py:67
  25.5 0.0 all-reduce.7.cloned.1.call-update
  25.6 0.0 all-reduce.5.cloned.1.call-start
  25.6 0.0 copy-done.1
  25.6 0.1 copy.78
  25.7 0.1 reshape_squeeze.7
  25.8 1.3 dynamic-slice
  27.2 199.2 %all-reduce.7.cloned.1.call-done = f32[64,1,3072]{2,0,1:T(8,128)} async-done(((f32[64,1,3072]{2,0,1:T(8,128)}), f32[64,1,3072]{2,0,1:T(8,128)}) %all-reduce.7.cloned.1.call-update) | async-done | bytes 786448
  226.4 1.6 convert_bitcast_fusion
  227.9 48.3 %all-gather = bf16[64,1,3072]{2,1,0:T(2,128)(2,1)S(1)} all-gather(bf16[1,1,3072]{2,1,0:T(2,128)(2,1)S(1)} %convert_bitcast_fusion), channel_id=1, replica_groups=mesh['tile'=64,'view'=8] {'tile'}, dimensions={0}, use_global_device_ids=true | all-gather | bytes 399360 | tf_op jit(solution)/shard_map/all_gather | solution.py:73
  276.3 1.3 convolution_convert_fusion
  277.6 2.3 copy.84
  279.9 3.1 copy.85
  283.0 2.7 fusion.55
  285.7 8.5 %fusion.7 = f32[64,16,256]{2,1,0:T(8,128)} fusion(f32[128,64,256]{2,1,0:T(8,128)S(1)} %fusion.55, s32[128]{0:T(128)S(1)} %eq.31), kind=kOutput, calls=%fused_computation.17 | convolution fusion | flops 402655232 | bytes 9437696 | tf_op jit(solution)/shard_map/sq,spx->pqx/dot_general | solution.py:81
  294.2 3.2 copy.87
  297.4 3.1 copy.88
  300.5 3.4 copy.89
  303.9 0.0 all-reduce.5.cloned.1.call-update
  303.9 2.5 fusion.54
  306.4 2.3 collective-permute-start
  308.7 3.5 collective-permute-start.1
  312.2 0.9 convert_reduce_fusion
  313.1 0.1 copy.90
  313.2 0.2 convolution_bitcast_fusion.1
  313.4 0.1 reshape.106
  313.5 30.9 %psum.15 = f32[8,512]{1,0:T(8,128)S(1)} all-reduce(f32[8,512]{1,0:T(8,128)S(1)} %reshape.106), channel_id=1, replica_groups=mesh['tile'=64,'view'=8] {'view'}, use_global_device_ids=true, to_apply=%region_3.4 | all-reduce | flops 4096 | bytes 32768 | tf_op jit(solution)/shard_map/psum | solution.py:106
  344.3 0.0 collective-permute-done
  344.3 0.0 collective-permute-done.1
  344.3 3.0 select_maximum_fusion
  347.3 38.9 %all-reduce.5.cloned.1.call-done = f32[64,8,512]{2,1,0:T(8,128)} async-done(((f32[64,8,512]{2,1,0:T(8,128)}), f32[64,8,512]{2,1,0:T(8,128)}) %all-reduce.5.cloned.1.call-update) | async-done | bytes 1048592 | tf_op jit(solution)/shard_map/psum | solution.py:106
  386.2 4.5 %fusion.14 = f32[64,8,512]{2,1,0:T(8,128)} fusion(f32[64,8,512]{2,1,0:T(8,128)} %param.5, f32[66,10,514]{2,1,0:T(8,128)S(1)} %select_maximum_fusion, f32[64,1,512]{2,1,0:T(1,128)S(1)} %collective-permute-done, f32[64,1,512]{2,1,0:T(1,128)S(1)} %collective-permute-done.1, f32[64,8,512]{2,1,0:T(8,128)} %all-reduce.5.cloned.1.call-done, f32[8,512]{1,0:T(8,128)S(1)} %psum.15), kind=kLoop, calls=%fused_computation.24 | loop fusion | flops 6029312 | bytes 7618560 | tf_op jit(solution)/shard_map/div | solution.py:107
  (1 shorter events, 0.0 us)
Async XLA Ops:
  6.5 219.8 %all-reduce.7.cloned.1.call-start = ((), (), s32[]{:S(2)}) async-start(), calls=%async_computation.1 | async-start | bytes 1572864
  11.0 2.5 copy-start
  17.9 3.4 copy-start.2
  21.2 4.5 %copy-start.1 = (f32[1,1,1,64,48]{3,4,2,1,0:T(8,128)S(1)}, f32[1,1,1,64,48]{3,4,2,1,0:T(8,128)}, u32[]{:S(2)}) copy-start(f32[1,1,1,64,48]{3,4,2,1,0:T(8,128)} %param.7) | copy-start | bytes 36868
  25.6 360.7 %all-reduce.5.cloned.1.call-start = ((), (), s32[]{:S(2)}) async-start(), calls=%async_computation | async-start | bytes 2097152 | tf_op jit(solution)/shard_map/psum | solution.py:106
  306.4 38.0 %collective-permute-start = (f32[64,1,512]{2,1,0:T(1,128)}, f32[64,1,512]{2,1,0:T(1,128)S(1)}, u32[]{:S(2)}, u32[]{:S(2)}) collective-permute-start(f32[64,1,512]{2,1,0:T(1,128)} %get-tuple-element.7), channel_id=1, source_target_pairs={{0,8},{8,16},{16,24},{24,32},{32,40},{40,48},{48,56},{56,64},{64,7... | collective-permute-start | bytes 393224 | tf_op jit(solution)/shard_map/ppermute | solution.py:17
  308.7 35.7 %collective-permute-start.1 = (f32[64,1,512]{2,1,0:T(1,128)}, f32[64,1,512]{2,1,0:T(1,128)S(1)}, u32[]{:S(2)}, u32[]{:S(2)}) collective-permute-start(f32[64,1,512]{2,1,0:T(1,128)} %get-tuple-element.8), channel_id=1, source_target_pairs={{8,0},{16,8},{24,16},{32,24},{40,32},{48,40},{56,48},{64,56},{72,6... | collective-permute-start | bytes 393224 | tf_op jit(solution)/shard_map/ppermute | solution.py:18
Sparse Core Ops, SparseCore 0:
  25.7 200.6 all-reduce.6
  304.0 82.1 all-reduce.4
where the time goes:
time: 398 us
  waiting for transfers between devices  238 us (60%)
  blocking collectives  79.2 us (20%)
  local copies, waits for them, and re-layouts  27.2 us (7%)
  matrix products  23.7 us (6%)
  between operations  13.5 us (3%)
  other arithmetic  9.96 us (3%)
  starting transfers between devices  5.81 us (1%)
    unnamed x3, waiting for transfers between devices  199 us
    all_gather x1, blocking collectives, per_device(): every_block = lax.all_gather(ratios, 'tile', axis=0, tiled=True)  48.3 us
    psum x1, waiting for transfers between devices, per_device(): back_total, sens_total = lax.psum((back_sum, sensitivity), 'view')  38.9 us
    psum x1, blocking collectives, per_device(): back_total, sens_total = lax.psum((back_sum, sensitivity), 'view')  30.9 us
    dot_general x1, matrix products, per_device(): jnp.einsum('sq,spx->pqx', segment_onehot, spread_back, precision=high)  8.51 us
  transfers between devices with their start and end apart: 4, of which 2 were waited for; matrix products, arithmetic and copies ran while one was open for 2% of the time, Pallas kernels for 0%

commit v1 on v0

--- a/solution.py
+++ b/solution.py
@@ -1,3 +1,4 @@
+import functools
 import jax
 import jax.numpy as jnp
 from jax import lax
@@ -5,6 +6,16 @@
 
 BACKGROUND = 1.0
 HUBER_DELTA = 0.1
+
+
+def remake_matrix(local_array, axis_id, at_axis):
+    newest = lax.axis_size(axis_id)
+    res = jnp.stack(newest * [local_array], 0)
+    now = lax.all_to_all(res, axis_name=axis_id, split_axis=0, concat_axis=0)
+    return jnp.concatenate(now, at_axis)
+
+
+bands_divide = functools.partial(remake_matrix, axis_id="tile", at_axis=0)
 
 
 def extended(x, sides, width):
@@ -70,7 +81,7 @@
     ratios = (measured[0, 0].reshape(owned, flat_width) / (projection + BACKGROUND)).astype(
         jnp.bfloat16
     )
-    every_block = lax.all_gather(ratios, "tile", axis=0, tiled=True)
+    every_block = bands_divide(ratios)
     picked = jnp.dot(
         block_onehot.astype(jnp.bfloat16), every_block, preferred_element_type=jnp.float32
     ).astype(jnp.bfloat16)

time: 398 us -> 383 us (0.962)
  blocking collectives: 79.2 us -> 54 us
  local copies, waits for them, and re-layouts: 27.2 us -> 33.9 us
  other arithmetic: 9.96 us -> 14.8 us
    all_gather x1 -> x0, blocking collectives: 48.3 us -> none  [per_device(): every_block = lax.all_gather(ratios, 'tile', axis=0, tiled=True)]
    all_to_all x0 -> x1, blocking collectives: none -> 23.2 us  [remake_matrix(): now = lax.all_to_all(res, axis_name=axis_id, split_axis=0, concat_axis=0)]
    unnamed x9 -> x11, local copies, waits for them, and re-layouts: 3.22 us -> 8.05 us
    another operation x0 -> x1, other arithmetic: none -> 4.66 us  [remake_matrix(): res = jnp.stack(newest * [local_array], 0)]
where the time goes in v1:
time: 383 us; the launch traced here: 382 us
  waiting for transfers between devices  235 us (61%)
  blocking collectives  54 us (14%)
  local copies, waits for them, and re-layouts  33.9 us (9%)
  matrix products  24.8 us (6%)
  other arithmetic  14.8 us (4%)
  between operations  13.5 us (4%)
  starting transfers between devices  5.81 us (2%)
    unnamed x3, waiting for transfers between devices  199 us
    psum x1, waiting for transfers between devices, per_device(): back_total, sens_total = lax.psum((back_sum, sensitivity), 'view')  36.2 us
    psum x1, blocking collectives, per_device(): back_total, sens_total = lax.psum((back_sum, sensitivity), 'view')  30.9 us
    all_to_all x1, blocking collectives, remake_matrix(): now = lax.all_to_all(res, axis_name=axis_id, split_axis=0, concat_axis=0)  23.2 us
    dot_general x1, matrix products, per_device(): jnp.einsum('sq,spx->pqx', segment_onehot, spread_back, precision=high)  8.51 us
    unnamed x11, local copies, waits for them, and re-layouts  8.05 us
  transfers between devices with their start and end apart: 4, of which 2 were waited for; matrix products, arithmetic and copies ran while one was open for 2% of the time, Pallas kernels for 0%

profile of v1, /device:TPU:2, one launch (start us, length us, event | category | flops | bytes accessed | tf_op | source)
XLA Modules:
  0.0 382.4 jit_solution(3134934610237096411)
XLA Ops:
  6.5 0.0 all-reduce.7.cloned.1.call-start
  6.5 0.8 slice_reduce_fusion.1
  7.3 0.1 eq.31
  7.4 1.8 copy.83
  9.2 0.1 copy.84
  9.3 1.6 copy.85
  11.0 0.0 copy-start
  11.0 2.5 convolution_convert_fusion.1
  13.4 0.0 copy-done
  13.4 4.5 %fusion.2 = f32[128,64,48]{1,2,0:T(8,128)} fusion(bf16[128,48,256]{2,1,0:T(8,128)(2,1)S(1)} %bitcast.51, bf16[128,64,256]{2,0,1:T(8,128)(2,1)S(1)} %convolution_convert_fusion.1), kind=kOutput, calls=%fused_computation.3 | convolution fusion | flops 201326592 | bytes 8912896 | tf_op jit(solution)/shard_map/spx,snx->spn/dot_general | solution.py:75
  17.9 0.0 copy-start.2
  17.9 3.3 copy.87
  21.2 0.0 copy-start.1
  21.2 0.1 reshape_squeeze.6
  21.3 0.0 copy-done.2
  21.3 0.1 fusion.48
  21.3 0.1 reshape.92
  21.4 4.1 %convolution_bitcast_fusion = f32[64,1,3072]{2,0,1:T(8,128)} fusion(f32[128,3072]{0,1:T(8,128)} %bitcast.55, f32[128]{0:T(128)S(1)} %reshape.92, s32[128]{0:T(128)S(1)} %fusion.50), kind=kOutput, calls=%fused_computation.10 | convolution fusion | flops 302006272 | bytes 2360320 | tf_op jit(solution)/shard_map/dot_general | solution.py:78
  25.5 0.0 all-reduce.7.cloned.1.call-update
  25.6 0.0 all-reduce.5.cloned.1.call-start
  25.6 0.0 copy-done.1
  25.6 0.1 copy.82
  25.7 0.1 reshape_squeeze.7
  25.8 1.3 dynamic-slice
  27.2 199.2 %all-reduce.7.cloned.1.call-done = f32[64,1,3072]{2,0,1:T(8,128)} async-done(((f32[64,1,3072]{2,0,1:T(8,128)}), f32[64,1,3072]{2,0,1:T(8,128)}) %all-reduce.7.cloned.1.call-update) | async-done | bytes 786448
  226.4 1.6 convert_reduce_fusion.1
  228.0 1.3 stack.5
  229.3 0.6 broadcast.92
  229.8 4.7 %reduce.11 = bf16[64,3072]{1,0:T(8,128)(2,1)} reduce(bf16[64,1,3072]{2,1,0:T(2,128)(2,1)} %stack.5, bf16[]{:T(256)} %broadcast.92), dimensions={1}, to_apply=%stack.5.reduce_sub_computation | reduce | bytes 786434 | tf_op jit(solution)/shard_map/stack | solution.py:13
  234.5 1.3 reshape.112
  235.8 23.2 %all_to_all.5 = bf16[64,2,1536]{2,1,0:T(2,128)(2,1)} all-to-all(bf16[64,2,1536]{2,1,0:T(2,128)(2,1)S(1)} %reshape.112), channel_id=1, replica_groups=mesh['tile'=64,'view'=8] {'tile'}, dimensions={0} | all-to-all | bytes 786432 | tf_op jit(solution)/shard_map/all_to_all | solution.py:14
  258.9 3.5 reshape.113
  262.5 2.4 convolution_convert_fusion
  264.9 2.3 copy.89
  267.2 3.1 copy.90
  270.3 2.7 fusion.55
  273.0 8.5 %fusion.7 = f32[64,16,256]{2,1,0:T(8,128)} fusion(f32[128,64,256]{2,1,0:T(8,128)S(1)} %fusion.55, s32[128]{0:T(128)S(1)} %eq.31), kind=kOutput, calls=%fused_computation.17 | convolution fusion | flops 402655232 | bytes 9437696 | tf_op jit(solution)/shard_map/sq,spx->pqx/dot_general | solution.py:92
  281.5 3.2 copy.92
  284.7 3.1 copy.93
  287.8 3.4 copy.94
  291.2 0.0 all-reduce.5.cloned.1.call-update
  291.2 2.5 fusion.54
  293.7 2.1 collective-permute-start
  295.8 3.7 collective-permute-start.1
  299.5 0.9 convert_reduce_fusion
  300.4 0.1 copy.95
  300.5 0.2 convolution_bitcast_fusion.1
  300.7 0.1 reshape.91
  300.8 30.9 %psum.15 = f32[8,512]{1,0:T(8,128)S(1)} all-reduce(f32[8,512]{1,0:T(8,128)S(1)} %reshape.91), channel_id=1, replica_groups=mesh['tile'=64,'view'=8] {'view'}, use_global_device_ids=true, to_apply=%region_3.4 | all-reduce | flops 4096 | bytes 32768 | tf_op jit(solution)/shard_map/psum | solution.py:117
  331.7 0.0 collective-permute-done
  331.7 0.0 collective-permute-done.1
  331.7 3.0 select_maximum_fusion
  334.7 36.2 %all-reduce.5.cloned.1.call-done = f32[64,8,512]{2,1,0:T(8,128)} async-done(((f32[64,8,512]{2,1,0:T(8,128)}), f32[64,8,512]{2,1,0:T(8,128)}) %all-reduce.5.cloned.1.call-update) | async-done | bytes 1048592 | tf_op jit(solution)/shard_map/psum | solution.py:117
  370.9 4.7 %fusion.14 = f32[64,8,512]{2,1,0:T(8,128)} fusion(f32[64,8,512]{2,1,0:T(8,128)} %param.5, f32[66,10,514]{2,1,0:T(8,128)S(1)} %select_maximum_fusion, f32[64,1,512]{2,1,0:T(1,128)S(1)} %collective-permute-done, f32[64,1,512]{2,1,0:T(1,128)S(1)} %collective-permute-done.1, f32[64,8,512]{2,1,0:T(8,128)} %all-reduce.5.cloned.1.call-done, f32[8,512]{1,0:T(8,128)S(1)} %psum.15), kind=kLoop, calls=%fused_computation.24 | loop fusion | flops 6029312 | bytes 7618560 | tf_op jit(solution)/shard_map/div | solution.py:118
  (1 shorter events, 0.0 us)
Async XLA Ops:
  6.5 219.8 %all-reduce.7.cloned.1.call-start = ((), (), s32[]{:S(2)}) async-start(), calls=%async_computation.2 | async-start | bytes 1572864
  11.0 2.5 copy-start
  17.9 3.4 copy-start.2
  21.2 4.5 %copy-start.1 = (f32[1,1,1,64,48]{3,4,2,1,0:T(8,128)S(1)}, f32[1,1,1,64,48]{3,4,2,1,0:T(8,128)}, u32[]{:S(2)}) copy-start(f32[1,1,1,64,48]{3,4,2,1,0:T(8,128)} %param.7) | copy-start | bytes 36868
  25.6 345.3 %all-reduce.5.cloned.1.call-start = ((), (), s32[]{:S(2)}) async-start(), calls=%async_computation.1 | async-start | bytes 2097152 | tf_op jit(solution)/shard_map/psum | solution.py:117
  293.7 38.0 %collective-permute-start = (f32[64,1,512]{2,1,0:T(1,128)}, f32[64,1,512]{2,1,0:T(1,128)S(1)}, u32[]{:S(2)}, u32[]{:S(2)}) collective-permute-start(f32[64,1,512]{2,1,0:T(1,128)} %get-tuple-element.7), channel_id=1, source_target_pairs={{0,8},{8,16},{16,24},{24,32},{32,40},{40,48},{48,56},{56,64},{64,7... | collective-permute-start | bytes 393224 | tf_op jit(solution)/shard_map/ppermute | solution.py:28
  295.8 35.9 %collective-permute-start.1 = (f32[64,1,512]{2,1,0:T(1,128)}, f32[64,1,512]{2,1,0:T(1,128)S(1)}, u32[]{:S(2)}, u32[]{:S(2)}) collective-permute-start(f32[64,1,512]{2,1,0:T(1,128)} %get-tuple-element.8), channel_id=1, source_target_pairs={{8,0},{16,8},{24,16},{32,24},{40,32},{48,40},{56,48},{64,56},{72,6... | collective-permute-start | bytes 393224 | tf_op jit(solution)/shard_map/ppermute | solution.py:29
Sparse Core Ops, SparseCore 0:
  25.7 200.6 all-reduce.6
  291.3 79.4 all-reduce.4
